TPU v7x, 32 devices: a whole 2x2x4 slice. The times are simulated.
32 devices in a mesh: member: 2 (over x), tile: 16 (over z, y, core).
Axes of the slice: x: 2, y: 2, z: 4, core: 2. Of those that a mesh axis runs over, the one named last changes fastest.
Arguments:
- precip: float32 [1024, 128], P(('member', 'tile')), parts along dimension 0, may hold values from 0.2 to 2
- pet: float32 [1024, 128], P(('member', 'tile')), parts along dimension 0, may hold values from 0.05 to 0.5
- soil_init: float32 [1024, 128], P(('member', 'tile')), parts along dimension 0, may hold values from 0.05 to 0.4
- ksat: float32 [1024, 128], P(('member', 'tile')), parts along dimension 0, may hold values from 0.5 to 3
- land_mask: int32 [1024, 128], P(('member', 'tile')), parts along dimension 0, may hold values 0 or 1
- head_init: float32 [1024, 2048], P(('member', 'tile')), parts along dimension 0, may hold values from 0.2 to 2
- subsurface_init: float32 [1024, 2048], P(('member', 'tile')), parts along dimension 0, may hold values from 0.2 to 2
- conduct: float32 [1024, 2048], P(('member', 'tile')), parts along dimension 0, may hold values from 0.22 to 0.47
- drain_rate: float32 [1024, 2048], P(('member', 'tile')), parts along dimension 0, may hold values from 0.05 to 0.4
- flow_code: int32 [1024, 2048], P(('member', 'tile')), parts along dimension 0, may hold values from 0 to 3
- channel_share: float32 [1024, 2048], P(('member', 'tile')), parts along dimension 0, may hold values from 0.02 to 0.2
- cell_slot: int32 [1024, 2048], P(('member', 'tile')), parts along dimension 0, may hold values from 0 to 1023
- slot_reach: int32 [32768], P(('member', 'tile')), parts along dimension 0, may hold values from 0 to 1023
Outputs:
- soil: float32 [1024, 128], P(('member', 'tile')), parts along dimension 0
- head: float32 [1024, 2048], P(('member', 'tile')), parts along dimension 0
- subsurface: float32 [1024, 2048], P(('member', 'tile')), parts along dimension 0
- reach_inflow: float32 [32768], P(('member', 'tile')), parts along dimension 0
There are 2 independent parts, one for each index of `member`. A program takes and returns all parts, laid end to end along the dimension named above; each array names one. Nothing has to cross between parts.
Inputs may be any that keep to these rules, and one draw needn't show every extreme that they name: `slot_reach`: slot k of a tile holds a reach owned by tile index k // 64.
All inputs are finite; a program needn't handle non-finite values. No bound on the sum of `land_mask` on one device may be relied on, other than what follows from the above.
Results may differ from a plain program's by a relative error of at most 0.00002.
Values sent between devices are 32-bit elements; how exact they have to be, the bound alone decides.
A program may use at most 64 MiB of HBM per device.

v0:
```python
import functools

import jax
import jax.numpy as jnp
from jax import lax
from jax.experimental import pallas as pl
from jax.experimental.pallas import tpu as pltpu
from jax.sharding import PartitionSpec as P

ITERS = 6
HALO = 8
TILE = 8
LANES = 128
MESH = pl.DeviceIdType.MESH
NT = (((1,), (1,)), ((), ()))


def parts_of(x, count):
    parts = []
    for _ in range(count):
        part = x.astype(jnp.bfloat16)
        parts.append(part)
        x = x - part.astype(jnp.float32)
    return parts


def kernel(
    n,
    precip,
    pet,
    soil_init,
    ksat,
    land_mask,
    head_init,
    subsurface_init,
    conduct,
    drain_rate,
    flow_code,
    channel_share,
    cell_slot,
    slot_reach,
    soil_out,
    head_out,
    sub_out,
    reach_out,
    land_in,
    mask_in,
    pack,
    land_send,
    land_recv,
    wide,
    h,
    s,
    g,
    d,
    code,
    share_v,
    slot_v,
    fields,
    statics,
    inverse,
    ratio,
    final,
    values,
    keys,
    owner_hot,
    spot_hot,
    sums_send,
    sums_recv,
    places,
    spots,
    middle,
    land_sem,
    own_sem,
    halo_sem,
    a2a_send,
    a2a_recv,
):
    me = lax.axis_index("tile")
    cols, land_rows = precip.shape
    rows, width = head_init.shape
    full = rows + 2 * HALO
    chunks = width // LANES
    land_dev = land_rows // n
    per_chunk = LANES // (width // n)
    per_owner = slot_reach.shape[0] * LANES // n
    twins = LANES // per_owner
    reach_rows = reach_out.shape[0]
    tall = ((head_init, h), (conduct, g), (subsurface_init, s), (drain_rate, d), (flow_code, code))
    urgent, patient = (0, 1), (2, 3, 4)
    states = [fields.at[i] for i in range(6)]
    water, store = states[0], states[3]
    half_way = ITERS // 2
    cond, sides, square, keep_h, keep_s, down_v, up_v, from_left, from_right = (
        statics.at[i] for i in range(9)
    )
    high_v, rest_v = values.at[0], values.at[1]
    owner_v, spot_v = keys.at[0], keys.at[1]

    land_copies = [
        pltpu.make_async_copy(ref, land_in.at[i], land_sem.at[0])
        for i, ref in enumerate((precip, pet, soil_init, ksat))
    ]
    land_copies.append(pltpu.make_async_copy(land_mask, mask_in, land_sem.at[1]))
    for copy in land_copies:
        copy.start()

    barrier = pltpu.get_barrier_semaphore()
    for k in range(1, n):
        pl.semaphore_signal(
            barrier, inc=1, device_id={"tile": lax.rem(me + k, n)}, device_id_type=MESH
        )

    own = [
        pltpu.make_async_copy(src, dst.at[pl.ds(HALO, rows)], own_sem.at[i])
        for i, (src, dst) in enumerate(tall)
    ]
    own.append(pltpu.make_async_copy(channel_share, share_v, own_sem.at[5]))
    own.append(pltpu.make_async_copy(cell_slot, slot_v, own_sem.at[6]))
    own.append(pltpu.make_async_copy(slot_reach.at[me // twins], places.at[me], own_sem.at[7]))
    for copy in own:
        copy.start()

    @pl.when(me == 0)
    def _():
        for _, dst in tall:
            dst[:HALO, :] = jnp.zeros((HALO, width), dst.dtype)
        middle[0] = jnp.zeros(middle.shape[1:], jnp.float32)

    @pl.when(me == n - 1)
    def _():
        for _, dst in tall:
            dst[full - HALO :, :] = jnp.zeros((HALO, width), dst.dtype)
        middle[1] = jnp.zeros(middle.shape[1:], jnp.float32)

    land_copies[-1].wait()
    pltpu.make_async_copy(land_in, land_in, land_sem.at[0]).wait()
    rain, demand, moist, conductivity = land_in[0], land_in[1], land_in[2], land_in[3]
    mask = mask_in[...].astype(jnp.float32)
    wet = 2.0 * moist
    cap = conductivity * (1.0 - wet)
    runoff = mask * rain * rain / (rain + cap)
    drainage = 0.25 * mask * conductivity * (wet * wet) * (wet * wet)
    evap = mask * demand * wet
    soil_out[...] = moist + 0.1 * (mask * rain - runoff - drainage - evap)
    lane = lax.broadcasted_iota(jnp.int32, (cols, land_rows), 1)
    place = lax.rem(lane, land_dev)
    side = HALO // 4
    if 4 * cols < LANES:
        pack[4 * cols :, :] = jnp.zeros((LANES - 4 * cols, land_rows), jnp.float32)
    for i, x in enumerate((runoff, drainage)):
        pack[i * cols : (i + 1) * cols, :] = x
        before = jnp.where(lane >= land_dev, pltpu.roll(x, side, 1), 0.0)
        after = jnp.where(
            lane < land_rows - land_dev, pltpu.roll(x, land_rows - (land_dev - side), 1), 0.0
        )
        pack[(2 + i) * cols : (3 + i) * cols, :] = jnp.where(place < side, before, after)
    land_send[...] = jnp.transpose(pack[...]).reshape(n, land_dev, LANES)

    def drain(ref, sem):
        pltpu.make_async_copy(ref, ref, sem).wait()

    def to_peers(stage, source, target):
        for k in range(1, n):
            peer = lax.rem(me + jnp.where(me < n // 2, n - k, k), n)
            pltpu.make_async_remote_copy(
                src_ref=source(peer),
                dst_ref=target,
                send_sem=a2a_send.at[stage],
                recv_sem=a2a_recv.at[stage],
                device_id={"tile": peer},
                device_id_type=MESH,
            ).start()

    def at(c):
        return pl.ds(c * LANES, LANES)

    lane8 = lax.broadcasted_iota(jnp.int32, (TILE, LANES), 1)
    first = lane8 == 0
    last = lane8 == LANES - 1
    top8 = lax.broadcasted_iota(jnp.int32, (TILE, LANES), 0) < TILE // 2
    zero = jnp.zeros((TILE, LANES), jnp.float32)

    def rolled(x):
        return (pltpu.roll(x, 1, 1), pltpu.roll(x, LANES - 1, 1))

    def prepare_water(m):
        band = pl.ds(TILE * m, TILE)

        def load(c):
            gc = g[band, at(c)]
            cond[c, band, :] = gc
            square[c, band, :] = gc * gc
            return rolled(gc)

        before, here = (zero,) * 2, load(0)
        for c in range(chunks):
            after = load(c + 1) if c + 1 < chunks else (zero,) * 2
            sides[c, band, :] = jnp.where(first, before[0], here[0]) + jnp.where(last, after[1], here[1])
            before, here = here, after

    def prepare_store(m):
        band = pl.ds(TILE * m, TILE)

        def load(c):
            dc, kc = d[band, at(c)], code[band, at(c)]
            down, up, right, left = (jnp.where(kc == q, dc, 0.0) for q in range(4))
            keep_s[c, band, :] = 1.0 - (down + up + right + left)
            down_v[c, band, :] = down
            up_v[c, band, :] = up
            return (pltpu.roll(right, 1, 1), pltpu.roll(left, LANES - 1, 1))

        before, here = (zero,) * 2, load(0)
        for c in range(chunks):
            after = load(c + 1) if c + 1 < chunks else (zero,) * 2
            from_left[c, band, :] = jnp.where(first, before[0], here[0])
            from_right[c, band, :] = jnp.where(last, after[1], here[1])
            before, here = here, after

    def finish(start):
        band, above, below = (pl.ds(start + q, TILE) for q in (0, -1, 1))
        for c in range(chunks):
            around = (cond[c, above, :] + cond[c, below, :]) + sides[c, band, :]
            keep_h[c, band, :] = 1.0 - cond[c, band, :] * around

    line = lax.broadcasted_iota(jnp.int32, (16, LANES), 0).astype(jnp.float32)
    lines = [(line + 16 * q).astype(jnp.bfloat16) for q in range(max(n, per_owner) // 16)]
    one, none = jnp.ones((16, LANES), jnp.bfloat16), jnp.zeros((16, LANES), jnp.bfloat16)

    def row_of(ref, c, r):
        half = ref[c, pl.ds(r, TILE, stride=0), :]
        return jnp.concatenate([half, half], axis=0).astype(jnp.bfloat16)

    def make_hot(r, carry):
        for ref, hot, count in ((owner_v, owner_hot, n), (spot_v, spot_hot, per_owner)):
            for c in range(chunks):
                key = row_of(ref, c, r)
                for q in range(count // 16):
                    hot[r, 16 * q : 16 * (q + 1), at(c)] = jnp.where(key == lines[q], one, none)
        return carry

    inner = range(1, 1 + rows // TILE)

    def local_work():
        for copy in own:
            copy.wait()
        for m in inner:
            prepare_water(m)
            prepare_store(m)
            band, own_band = pl.ds(TILE * m, TILE), pl.ds(TILE * (m - 1), TILE)
            for c in range(chunks):
                backward = 1.0 / g[band, at(c)]
                inverse[c, own_band, :] = backward
                ratio[c, own_band, :] = share_v[own_band, at(c)] * backward
                slot = slot_v[own_band, at(c)]
                owner = slot // per_owner
                owner_v[c, own_band, :] = owner.astype(jnp.float32)
                spot_v[c, own_band, :] = (slot - owner * per_owner).astype(jnp.float32)
        for start in (*range(HALO + 1, HALO + rows - TILE, TILE), HALO + rows - TILE - 1):
            finish(start)
        lax.fori_loop(0, rows, make_hot, 0)

    @pl.when(me < n // 2)
    def _():
        local_work()

    pl.semaphore_wait(barrier, n - 1)
    own_land = land_recv.at[lax.rem(me, per_chunk), me // per_chunk]
    to_peers(0, lambda peer: land_send.at[peer], own_land)

    def halo_copy(i, up):
        src, dst = tall[i]
        if up:
            start, land, peer = (rows - half_way, HALO - half_way, me + 1)
        else:
            start, land, peer = (0, full - HALO, me - 1)
        return pltpu.make_async_remote_copy(
            src_ref=src.at[pl.ds(start, half_way)],
            dst_ref=dst.at[pl.ds(land, half_way)],
            send_sem=halo_sem.at[(0 if up else 1) + (0 if i in urgent else 12)],
            recv_sem=halo_sem.at[(2 if up else 3) + (0 if i in urgent else 12)],
            device_id={"tile": lax.rem(peer + n, n)},
            device_id_type=MESH,
        )

    def send_halo(which):
        @pl.when(me < n - 1)
        def _():
            for i in which:
                halo_copy(i, True).start()

        @pl.when(me > 0)
        def _():
            for i in which:
                halo_copy(i, False).start()

    send_halo(urgent)
    send_halo(patient)
    to_peers(1, lambda peer: slot_reach.at[peer // twins], places.at[me])
    land_recv[lax.rem(me, per_chunk), me // per_chunk] = land_send[me]

    @pl.when(me >= n // 2)
    def _():
        local_work()

    def take_halo(which):
        shift = 0 if which is urgent else 12
        size = water.at[:, pl.ds(0, len(which) * half_way), :]

        @pl.when(me > 0)
        def _():
            drain(size, halo_sem.at[2 + shift])

        @pl.when(me < n - 1)
        def _():
            drain(size, halo_sem.at[3 + shift])

    take_halo(urgent)
    outer = (0, full // TILE - 1)
    for m in outer:
        prepare_water(m)
    for start in (1, HALO + rows - 1):
        finish(start)

    drain(land_send.at[pl.ds(0, n - 1)], a2a_send.at[0])
    drain(land_send.at[pl.ds(0, n - 1)], a2a_recv.at[0])

    l_iota = lax.broadcasted_iota(jnp.int32, (LANES, 4 * LANES), 0)
    f_iota = lax.broadcasted_iota(jnp.int32, (LANES, 4 * LANES), 1)
    cell = lax.rem(f_iota, LANES) // 4
    group = f_iota // LANES
    total = None
    for k in range(per_chunk):
        inside = (cell >= k * cols) & (cell < (k + 1) * cols)
        spread = inside & (l_iota == group * cols + cell - k * cols)
        spread = jnp.where(spread, 1.0, 0.0).astype(jnp.bfloat16)
        block = land_recv[k].reshape(chunks * land_dev, LANES)
        for part in parts_of(block, 3):
            term = jnp.dot(part, spread, preferred_element_type=jnp.float32)
            total = term if total is None else total + term
    wide[...] = total

    def fill(m, i):
        band = pl.ds(TILE * m, TILE)
        for c in range(chunks):
            pair = []
            for q in (2 * m, 2 * m + 1):
                if q < side:
                    lanes, r = (2 + i) * LANES, q
                elif q < side + land_dev:
                    lanes, r = i * LANES, q - side
                else:
                    lanes, r = (2 + i) * LANES, q - land_dev
                r = c * land_dev + r
                pair.append(jnp.broadcast_to(wide[r : r + 1, lanes : lanes + LANES], (TILE, LANES)))
            added = jnp.where(top8, pair[0], pair[1])
            if i == 0:
                water[c, band, :] = g[band, at(c)] * (h[band, at(c)] + added)
            else:
                store[c, band, :] = s[band, at(c)] + added

    for m in (*outer, *inner):
        fill(m, 0)

    def advance_water(w, start, put):
        def load(c):
            wc = w[c, pl.ds(start, TILE), :]
            return (wc,) + rolled(wc)

        band, above, below = (pl.ds(start + q, TILE) for q in (0, -1, 1))
        before, here = (zero,) * 3, load(0)
        for c in range(chunks):
            after = load(c + 1) if c + 1 < chunks else (zero,) * 3
            flux = jnp.where(first, before[1], here[1]) + jnp.where(last, after[2], here[2])
            flux = flux + (w[c, above, :] + w[c, below, :])
            put(c, keep_h[c, band, :] * here[0] + square[c, band, :] * flux)
            before, here = here, after

    def advance_store(t, start, put):
        def load(c):
            tc = t[c, pl.ds(start, TILE), :]
            return (tc,) + rolled(tc)

        band, above, below = (pl.ds(start + q, TILE) for q in (0, -1, 1))
        before, here = (zero,) * 3, load(0)
        for c in range(chunks):
            after = load(c + 1) if c + 1 < chunks else (zero,) * 3
            moved = from_left[c, band, :] * jnp.where(first, before[1], here[1])
            moved = moved + from_right[c, band, :] * jnp.where(last, after[2], here[2])
            moved = moved + (down_v[c, above, :] * t[c, above, :] + up_v[c, below, :] * t[c, below, :])
            put(c, keep_s[c, band, :] * here[0] + moved)
            before, here = here, after

    top, end = HALO, HALO + rows
    later = ITERS - half_way - 1
    path = ((1, 0, 2), (4, 3, 5))

    def substep(advance, source, target, starts):
        for start in starts:

            def put(c, new):
                states[target][c, pl.ds(start, TILE), :] = new

            advance(states[source], start, put)

    def middle_copy(i, down):
        start = end - half_way if down else top
        return pltpu.make_async_remote_copy(
            src_ref=fields.at[path[i][0], :, pl.ds(start, half_way), :],
            dst_ref=middle.at[0 if down else 1, i],
            send_sem=halo_sem.at[4 + 2 * i + (0 if down else 1)],
            recv_sem=halo_sem.at[8 + 2 * i + (0 if down else 1)],
            device_id={"tile": lax.rem(me + (1 if down else n - 1), n)},
            device_id_type=MESH,
        )

    def first_half(i, advance):
        source, target = 3 * i, 3 * i + 1
        for reach in range(half_way - 1, 0, -1):
            substep(advance, source, target, range(top - reach, end + reach, TILE))
            source, target = target, source
        substep(advance, source, target, (top, end - TILE))

        @pl.when(me < n - 1)
        def _():
            middle_copy(i, True).start()

        @pl.when(me > 0)
        def _():
            middle_copy(i, False).start()

        substep(advance, source, target, range(top + TILE, end - TILE, TILE))

    def take_middle(i):
        @pl.when(me > 0)
        def _():
            middle_copy(i, True).wait_recv()

        @pl.when(me < n - 1)
        def _():
            middle_copy(i, False).wait_recv()

        for c in range(chunks):
            states[path[i][0]][c, top - half_way : top, :] = middle[0, i, c]
            states[path[i][0]][c, end : end + half_way, :] = middle[1, i, c]

    def edges(i, advance):
        for q in range(later):
            reach = later - q
            substep(advance, path[i][q], path[i][q + 1], (top - reach, end - TILE + reach))

    def last_water(starts):
        for start in starts:
            band = pl.ds(start - HALO, TILE)

            def put(c, new):
                final[c, band, :] = new
                taken = new * ratio[c, band, :]
                high = taken.astype(jnp.bfloat16).astype(jnp.float32)
                high_v[c, band, :] = high
                rest_v[c, band, :] = taken - high

            advance_water(states[path[0][later]], start, put)

    def last_store(starts):
        for start in starts:
            band = pl.ds(start - HALO, TILE)

            def put(c, new):
                sub_out[band, at(c)] = new

            advance_store(states[path[1][later]], start, put)

    first_half(0, advance_water)
    for q in range(later):
        reach = later - q
        substep(advance_water, path[0][q], path[0][q + 1], range(top + TILE - reach, end - TILE + reach, TILE))
    last_water(range(top + TILE, end - TILE, TILE))

    def add_row(r, total):
        hot = owner_hot[r]
        left = []
        for ref in (high_v, rest_v):
            row = jnp.concatenate([row_of(ref, c, r) for c in range(chunks)], axis=1)
            left += [hot[16 * q : 16 * (q + 1)] * row for q in range(n // 16)]
        left = jnp.concatenate(left, axis=0)
        return total + lax.dot_general(left, spot_hot[r], NT, preferred_element_type=jnp.float32)

    total = jnp.zeros((2 * n, per_owner), jnp.float32)
    total = lax.fori_loop(TILE, rows - TILE, add_row, total, unroll=8)
    take_middle(0)
    edges(0, advance_water)
    last_water((top, end - TILE))

    def add_wrapped(r, total):
        return add_row(lax.rem(r, rows), total)

    total = lax.fori_loop(rows - TILE, rows + TILE, add_wrapped, total, unroll=8)
    sums = total[:n] + total[n:]
    sums = jnp.concatenate([sums] * twins, axis=1)
    for k in range(n):
        sums_send[k] = sums[k : k + 1, :]
    sums_recv[me] = sums_send[me]
    to_peers(2, lambda peer: sums_send.at[peer], sums_recv.at[me])

    take_halo(patient)
    for m in outer:
        prepare_store(m)
    for m in (*outer, *inner):
        fill(m, 1)
    first_half(1, advance_store)
    for q in range(later):
        reach = later - q
        substep(advance_store, path[1][q], path[1][q + 1], range(top + TILE - reach, end - TILE + reach, TILE))
    last_store(range(top + TILE, end - TILE, TILE))
    for m in range(rows // TILE):
        band = pl.ds(TILE * m, TILE)
        for c in range(chunks):
            depth = final[c, band, :] * inverse[c, band, :]
            head_out[band, at(c)] = depth - share_v[band, at(c)] * depth

    drain(places.at[pl.ds(0, n - 1)], a2a_send.at[1])
    drain(places.at[pl.ds(0, n - 1)], a2a_recv.at[1])
    half = lax.broadcasted_iota(jnp.int32, (1, LANES), 1) // per_owner == lax.rem(me, twins)
    lane_line = lax.broadcasted_iota(jnp.int32, (LANES, LANES), 0)
    reach_line = lax.broadcasted_iota(jnp.int32, (reach_rows, LANES), 0)
    for j in range(n):
        low = lax.rem(places[j], LANES)
        spots[:, at(j)] = jnp.where(half & (lane_line == low), 1.0, 0.0).astype(jnp.bfloat16)

    take_middle(1)
    edges(1, advance_store)
    last_store((top, end - TILE))

    @pl.when(me < n - 1)
    def _():
        drain(water.at[:, pl.ds(0, len(urgent) * half_way), :], halo_sem.at[0])
        drain(water.at[:, pl.ds(0, len(patient) * half_way), :], halo_sem.at[12])
        middle_copy(0, True).wait_send()
        middle_copy(1, True).wait_send()

    @pl.when(me > 0)
    def _():
        drain(water.at[:, pl.ds(0, len(urgent) * half_way), :], halo_sem.at[1])
        drain(water.at[:, pl.ds(0, len(patient) * half_way), :], halo_sem.at[13])
        middle_copy(0, False).wait_send()
        middle_copy(1, False).wait_send()

    drain(sums_send.at[pl.ds(0, n - 1)], a2a_send.at[2])
    drain(sums_send.at[pl.ds(0, n - 1)], a2a_recv.at[2])
    found = []
    for j in range(n):
        high = places[j] // LANES
        found.append(jnp.where(reach_line == high, sums_recv[j], 0.0))
    found = jnp.concatenate(parts_of(jnp.concatenate(found, axis=1), 3), axis=0)
    reach = lax.dot_general(found, spots[...], NT, preferred_element_type=jnp.float32)
    reach_out[...] = reach[:reach_rows] + reach[reach_rows : 2 * reach_rows] + reach[2 * reach_rows :]


def flush(*refs):
    count = (len(refs) - 1) // 2
    copies = [
        pltpu.make_async_copy(src, dst, refs[-1].at[i])
        for i, (src, dst) in enumerate(zip(refs[:count], refs[count:-1]))
    ]
    for copy in copies:
        copy.start()
    for copy in copies:
        copy.wait()


def local(*args):
    n = lax.axis_size("tile")
    precip, head_init, slot_reach = args[0], args[5], args[12]
    cols, land_rows = precip.shape
    rows, width = head_init.shape
    slots = slot_reach.shape[0]
    full = rows + 2 * HALO
    land_dev = land_rows // n
    per_chunk = LANES // (width // n)
    chunks = width // LANES
    per_owner = slots // n
    f32, i32, b16 = jnp.float32, jnp.int32, jnp.bfloat16
    tall = pltpu.VMEM((full, width), f32)
    anywhere = pl.BlockSpec(memory_space=pl.ANY)
    soil, head, sub, reach = pl.pallas_call(
        functools.partial(kernel, n),
        out_shape=(
            pltpu.VMEM(precip.shape, f32),
            pltpu.VMEM(head_init.shape, f32),
            pltpu.VMEM(head_init.shape, f32),
            pltpu.VMEM((slots // LANES, LANES), f32),
        ),
        in_specs=[anywhere] * 13,
        out_specs=(pl.BlockSpec(memory_space=pltpu.VMEM),) * 4,
        scratch_shapes=[
            pltpu.VMEM((4, cols, land_rows), f32),
            pltpu.VMEM((cols, land_rows), i32),
            pltpu.VMEM((LANES, land_rows), f32),
            pltpu.VMEM((n, land_dev, LANES), f32),
            pltpu.VMEM((per_chunk, chunks, land_dev, LANES), f32),
            pltpu.VMEM((chunks * land_dev, 4 * LANES), f32),
            tall,
            tall,
            tall,
            tall,
            pltpu.VMEM((full, width), i32),
            pltpu.VMEM((rows, width), f32),
            pltpu.VMEM((rows, width), i32),
            pltpu.VMEM((6, chunks, full + TILE, LANES), f32),
            pltpu.VMEM((9, chunks, full + TILE, LANES), f32),
            pltpu.VMEM((chunks, rows, LANES), f32),
            pltpu.VMEM((chunks, rows, LANES), f32),
            pltpu.VMEM((chunks, rows, LANES), f32),
            pltpu.VMEM((2, chunks, rows + TILE, LANES), f32),
            pltpu.VMEM((2, chunks, rows + TILE, LANES), f32),
            pltpu.VMEM((rows, n, width), b16),
            pltpu.VMEM((rows, per_owner, width), b16),
            pltpu.VMEM((n, 1, LANES), f32),
            pltpu.VMEM((n, 1, LANES), f32),
            pltpu.VMEM((n, 1, LANES), i32),
            pltpu.VMEM((LANES, n * LANES), b16),
            pltpu.VMEM((2, 2, chunks, ITERS // 2, LANES), f32),
            pltpu.SemaphoreType.DMA((2,)),
            pltpu.SemaphoreType.DMA((8,)),
            pltpu.SemaphoreType.DMA((16,)),
            pltpu.SemaphoreType.DMA((3,)),
            pltpu.SemaphoreType.DMA((3,)),
        ],
        compiler_params=pltpu.CompilerParams(
            collective_id=0,
            has_side_effects=True,
            vmem_limit_bytes=40 * 2**20,
        ),
        name="step",
    )(*[pltpu.with_memory_space_constraint(x, pltpu.HBM) for x in (*args[:12], slot_reach.reshape(slots // LANES, 1, LANES))])
    results = (soil, head, sub, reach)
    soil, head, sub, reach = pl.pallas_call(
        flush,
        out_shape=tuple(jax.ShapeDtypeStruct(x.shape, x.dtype) for x in results),
        in_specs=[pl.BlockSpec(memory_space=pltpu.VMEM)] * 4,
        out_specs=(anywhere,) * 4,
        scratch_shapes=[pltpu.SemaphoreType.DMA((4,))],
        compiler_params=pltpu.CompilerParams(vmem_limit_bytes=2**20),
        name="flush",
    )(*results)
    return soil, head, sub, reach.reshape(slots)


def solution(mesh):
    grid = P(("member", "tile"), None)
    line = P(("member", "tile"))
    return jax.shard_map(
        local,
        mesh=mesh,
        in_specs=(grid,) * 12 + (line,),
        out_specs=(grid, grid, grid, line),
        check_vma=False,
    )
```

profile of v0, /device:TPU:0, one launch (start us, length us, event | category | flops | bytes accessed | tf_op | source)
XLA Modules:
  0.0 21.2 jit_solution(5419911375736905542)
XLA Ops:
  0.6 19.7 %step.1 = (f32[32,128]{1,0:T(8,128)S(1)}, f32[32,2048]{1,0:T(8,128)S(1)}, f32[32,2048]{1,0:T(8,128)S(1)}, f32[8,128]{1,0:T(8,128)S(1)}) custom-call(f32[32,128]{1,0:T(8,128)} %precip.1, f32[32,128]{1,0:T(8,128)} %pet.1, f32[32,128]{1,0:T(8,128)} %soil_init.1, f32[32,128]{1,0:T(8,128)} %ksat.1, s32[32,128]{1,0:T(8,128)} %land_mask.1, f32[32,2048]{1,0:T(8,128)} %head_init.1, ...), custom_call_target="tpu_custom_call" | custom-call | tf_op jit(solution)/shard_map/step/pallas_call | solution.py:586
  20.4 0.8 %flush.1 = (f32[32,128]{1,0:T(8,128)}, f32[32,2048]{1,0:T(8,128)}, f32[32,2048]{1,0:T(8,128)}, f32[8,128]{1,0:T(8,128)}) custom-call(f32[32,128]{1,0:T(8,128)S(1)} %get-tuple-element.12.refs_0_, f32[32,2048]{1,0:T(8,128)S(1)} %get-tuple-element.13.refs_1_, f32[32,2048]{1,0:T(8,128)S(1)} %get-tuple-element.14.refs_2_, f32[8,128]{1,0:T(8,128)S(1)} %get-tuple-element.15.refs_3_), custom_call_target="tpu_custom_call" | custom-call | tf_op jit(solution)/shard_map/flush/pallas_call | solution.py:638
where the time goes:
time: 21.4 us; the launch traced here: 21.2 us
  Pallas kernels  20.6 us (96%)
  between operations  0.64 us (3%)
    pallas_call x1, Pallas kernels, local(): pl.pallas_call(functools.partial(kernel, n), out_shape=(pltpu.VMEM(precip...  19.7 us
    pallas_call x1, Pallas kernels, local(): pl.pallas_call(flush, out_shape=tuple((jax.ShapeDtypeStruct(x.shape, x.dt...  0.83 us

commit v1 on v0

--- a/solution.py
+++ b/solution.py
@@ -42,7 +42,9 @@
     soil_out,
     head_out,
     sub_out,
-    reach_out,
+    sums_recv,
+    places,
+    spots,
     land_in,
     mask_in,
     pack,
@@ -66,9 +68,6 @@
     owner_hot,
     spot_hot,
     sums_send,
-    sums_recv,
-    places,
-    spots,
     middle,
     land_sem,
     own_sem,
@@ -85,7 +84,6 @@
     per_chunk = LANES // (width // n)
     per_owner = slot_reach.shape[0] * LANES // n
     twins = LANES // per_owner
-    reach_rows = reach_out.shape[0]
     tall = ((head_init, h), (conduct, g), (subsurface_init, s), (drain_rate, d), (flow_code, code))
     urgent, patient = (0, 1), (2, 3, 4)
     states = [fields.at[i] for i in range(6)]
@@ -523,7 +521,6 @@
     drain(places.at[pl.ds(0, n - 1)], a2a_recv.at[1])
     half = lax.broadcasted_iota(jnp.int32, (1, LANES), 1) // per_owner == lax.rem(me, twins)
     lane_line = lax.broadcasted_iota(jnp.int32, (LANES, LANES), 0)
-    reach_line = lax.broadcasted_iota(jnp.int32, (reach_rows, LANES), 0)
     for j in range(n):
         low = lax.rem(places[j], LANES)
         spots[:, at(j)] = jnp.where(half & (lane_line == low), 1.0, 0.0).astype(jnp.bfloat16)
@@ -548,23 +545,25 @@
 
     drain(sums_send.at[pl.ds(0, n - 1)], a2a_send.at[2])
     drain(sums_send.at[pl.ds(0, n - 1)], a2a_recv.at[2])
+
+
+def flush(soil, head, sub, sums, places, spots, soil_out, head_out, sub_out, reach_out, reach_v, sem):
+    copies = [
+        pltpu.make_async_copy(src, dst, sem.at[i])
+        for i, (src, dst) in enumerate(((head, head_out), (sub, sub_out), (soil, soil_out), (reach_v, reach_out)))
+    ]
+    for copy in copies[:-1]:
+        copy.start()
+    reach_rows = reach_v.shape[0]
+    reach_line = lax.broadcasted_iota(jnp.int32, (reach_rows, LANES), 0)
     found = []
-    for j in range(n):
+    for j in range(places.shape[0]):
         high = places[j] // LANES
-        found.append(jnp.where(reach_line == high, sums_recv[j], 0.0))
+        found.append(jnp.where(reach_line == high, sums[j], 0.0))
     found = jnp.concatenate(parts_of(jnp.concatenate(found, axis=1), 3), axis=0)
     reach = lax.dot_general(found, spots[...], NT, preferred_element_type=jnp.float32)
-    reach_out[...] = reach[:reach_rows] + reach[reach_rows : 2 * reach_rows] + reach[2 * reach_rows :]
-
-
-def flush(*refs):
-    count = (len(refs) - 1) // 2
-    copies = [
-        pltpu.make_async_copy(src, dst, refs[-1].at[i])
-        for i, (src, dst) in enumerate(zip(refs[:count], refs[count:-1]))
-    ]
-    for copy in copies:
-        copy.start()
+    reach_v[...] = reach[:reach_rows] + reach[reach_rows : 2 * reach_rows] + reach[2 * reach_rows :]
+    copies[-1].start()
     for copy in copies:
         copy.wait()
 
@@ -583,16 +582,18 @@
     f32, i32, b16 = jnp.float32, jnp.int32, jnp.bfloat16
     tall = pltpu.VMEM((full, width), f32)
     anywhere = pl.BlockSpec(memory_space=pl.ANY)
-    soil, head, sub, reach = pl.pallas_call(
+    results = pl.pallas_call(
         functools.partial(kernel, n),
         out_shape=(
             pltpu.VMEM(precip.shape, f32),
             pltpu.VMEM(head_init.shape, f32),
             pltpu.VMEM(head_init.shape, f32),
-            pltpu.VMEM((slots // LANES, LANES), f32),
+            pltpu.VMEM((n, 1, LANES), f32),
+            pltpu.VMEM((n, 1, LANES), i32),
+            pltpu.VMEM((LANES, n * LANES), b16),
         ),
         in_specs=[anywhere] * 13,
-        out_specs=(pl.BlockSpec(memory_space=pltpu.VMEM),) * 4,
+        out_specs=(pl.BlockSpec(memory_space=pltpu.VMEM),) * 6,
         scratch_shapes=[
             pltpu.VMEM((4, cols, land_rows), f32),
             pltpu.VMEM((cols, land_rows), i32),
@@ -617,9 +618,6 @@
             pltpu.VMEM((rows, n, width), b16),
             pltpu.VMEM((rows, per_owner, width), b16),
             pltpu.VMEM((n, 1, LANES), f32),
-            pltpu.VMEM((n, 1, LANES), f32),
-            pltpu.VMEM((n, 1, LANES), i32),
-            pltpu.VMEM((LANES, n * LANES), b16),
             pltpu.VMEM((2, 2, chunks, ITERS // 2, LANES), f32),
             pltpu.SemaphoreType.DMA((2,)),
             pltpu.SemaphoreType.DMA((8,)),
@@ -634,14 +632,16 @@
         ),
         name="step",
     )(*[pltpu.with_memory_space_constraint(x, pltpu.HBM) for x in (*args[:12], slot_reach.reshape(slots // LANES, 1, LANES))])
-    results = (soil, head, sub, reach)
     soil, head, sub, reach = pl.pallas_call(
         flush,
-        out_shape=tuple(jax.ShapeDtypeStruct(x.shape, x.dtype) for x in results),
-        in_specs=[pl.BlockSpec(memory_space=pltpu.VMEM)] * 4,
+        out_shape=(
+            *(jax.ShapeDtypeStruct(x.shape, x.dtype) for x in results[:3]),
+            jax.ShapeDtypeStruct((slots // LANES, LANES), f32),
+        ),
+        in_specs=[pl.BlockSpec(memory_space=pltpu.VMEM)] * 6,
         out_specs=(anywhere,) * 4,
-        scratch_shapes=[pltpu.SemaphoreType.DMA((4,))],
-        compiler_params=pltpu.CompilerParams(vmem_limit_bytes=2**20),
+        scratch_shapes=[pltpu.VMEM((slots // LANES, LANES), f32), pltpu.SemaphoreType.DMA((4,))],
+        compiler_params=pltpu.CompilerParams(vmem_limit_bytes=4 * 2**20),
         name="flush",
     )(*results)
     return soil, head, sub, reach.reshape(slots)

time: 21.4 us -> 21.2 us (level)
    pallas_call x1, Pallas kernels: 19.7 us -> 19.4 us  [local(): pl.pallas_call(functools.partial(kernel, n), out_shape=(pltpu.VMEM(precip...]
where the time goes in v1:
time: 21.2 us; the launch traced here: 21 us
  Pallas kernels  20.4 us (96%)
  between operations  0.64 us (3%)
    pallas_call x1, Pallas kernels, local(): pl.pallas_call(functools.partial(kernel, n), out_shape=(pltpu.VMEM(precip...  19.4 us
    pallas_call x1, Pallas kernels, local(): pl.pallas_call(flush, out_shape=(*(jax.ShapeDtypeStruct(x.shape, x.dtype)...  0.92 us

profile of v1, /device:TPU:0, one launch (start us, length us, event | category | flops | bytes accessed | tf_op | source)
XLA Modules:
  0.0 21.0 jit_solution(11971981529349578056)
XLA Ops:
  0.6 19.4 %step.1 = (f32[32,128]{1,0:T(8,128)S(1)}, f32[32,2048]{1,0:T(8,128)S(1)}, f32[32,2048]{1,0:T(8,128)S(1)}, f32[16,1,128]{2,1,0:T(1,128)S(1)}, s32[16,1,128]{2,1,0:T(1,128)S(1)}, /*index=5*/bf16[128,2048]{1,0:T(8,128)(2,1)S(1)}) custom-call(f32[32,128]{1,0:T(8,128)} %precip.1, f32[32,128]{1,0:T(8,128)} %pet.1, f32[32,128]{1,0:T(8,128)} %soil_init.1, ...), custom_call_target="tpu_custom_call" | custom-call | tf_op jit(solution)/shard_map/step/pallas_call | solution.py:585
  20.1 0.9 %flush.1 = (f32[32,128]{1,0:T(8,128)}, f32[32,2048]{1,0:T(8,128)}, f32[32,2048]{1,0:T(8,128)}, f32[8,128]{1,0:T(8,128)}) custom-call(f32[32,128]{1,0:T(8,128)S(1)} %get-tuple-element.14.soil, f32[32,2048]{1,0:T(8,128)S(1)} %get-tuple-element.15.head, f32[32,2048]{1,0:T(8,128)S(1)} %get-tuple-element.16.sub, f32[16,1,128]{2,1,0:T(1,128)S(1)} %get-tuple-element.17.sums, ...), custom_call_target="tpu_custom_call" | custom-call | tf_op jit(solution)/shard_map/flush/pallas_call | solution.py:635
